TPU v7x, 32 devices: a whole 2x2x4 slice. The times are simulated.
32 devices in a mesh: light: 4 (over x, core), strip: 8 (over z, y).
Axes of the slice: x: 2, y: 2, z: 4, core: 2. Of those that a mesh axis runs over, the one named last changes fastest.
Arguments:
- depth_start: float32 [128, 4096], P(None, 'strip'), may hold values from -0.3 to 0.3
- albedo_start: float32 [128, 4096], P(None, 'strip'), may hold values from 0.5 to 2
- observations: bfloat16 [32, 128, 4096], P('light', None, 'strip'), may hold values from 0 to 26
- light_table: int32 [32, 4], P('light'), may hold values from 0 to 999
- valid_mask: int32 [128, 4096], P(None, 'strip'), may hold values 0 or 1
Outputs:
- depth_final: float32 [128, 4096], P(None, 'strip')
- albedo_final: float32 [128, 4096], P(None, 'strip')
All inputs are finite; a program needn't handle non-finite values. No bound on the sum of `valid_mask` on one device may be relied on, other than what follows from the above.
Results may differ from a plain program's by a relative error of at most 0.0003.
Values may be sent and summed in bfloat16 or wider, within the bound.
No kernel may reach another device: no remote copies, remote signals or barrier semaphores. Data moves between devices by JAX's collectives and lax.ppermute only.
A program may use at most 64 MiB of HBM per device.

v0:
```python
import jax
import jax.numpy as jnp
from jax import lax
from jax.sharding import PartitionSpec as P

ITERS = 2
temper = 0.5
step_depth = 0.1
step_albedo = 0.2
epsilon = 1e-06


def extended(block, sides, width):
    for axis, dim in sides:
        count = lax.axis_size(axis)
        forward = [(i, i + 1) for i in range(count - 1)]
        backward = [(target, source) for source, target in forward]
        low = lax.ppermute(
            lax.slice_in_dim(block, block.shape[dim] - width, None, axis=dim), axis, forward
        )
        high = lax.ppermute(lax.slice_in_dim(block, 0, width, axis=dim), axis, backward)
        block = jnp.concatenate([low, block, high], axis=dim)
    return block


def decode_lights(table):
    values = table.astype(jnp.float32)
    light_x = (values[:, 0] / 500.0 - 1.0)[:, None, None]
    light_y = (values[:, 1] / 500.0 - 1.0)[:, None, None]
    light_z = (1.0 + values[:, 2] / 1000.0)[:, None, None]
    intensity = (0.5 + values[:, 3] / 1000.0)[:, None, None]
    return (light_x, light_y, light_z, intensity)


def shade_terms(surface, col_pad, row_pad, albedo, observed, table, valid, coord_x, coord_y):
    slope_x = 0.5 * (col_pad[:, 2:] - col_pad[:, :-2])
    slope_y = 0.5 * (row_pad[2:] - row_pad[:-2])
    light_x, light_y, light_z, intensity = decode_lights(table)
    delta_x = light_x - coord_x
    delta_y = light_y - coord_y
    delta_z = light_z - surface
    distance_sq = delta_x * delta_x + delta_y * delta_y + delta_z * delta_z
    norm_sq = 1.0 + slope_x * slope_x + slope_y * slope_y
    facing = -slope_x * delta_x - slope_y * delta_y + delta_z
    falloff = intensity / (distance_sq * jnp.sqrt(distance_sq) * jnp.sqrt(norm_sq))
    radiance = albedo * falloff * facing
    residual = valid * (radiance - observed.astype(jnp.float32))
    scores = -temper * residual * residual
    return (
        scores,
        residual,
        falloff,
        facing,
        delta_x,
        delta_y,
        delta_z,
        distance_sq,
        norm_sq,
        slope_x,
        slope_y,
    )


def light_gradients(weights, terms, albedo):
    (
        scores,
        residual,
        falloff,
        facing,
        delta_x,
        delta_y,
        delta_z,
        distance_sq,
        norm_sq,
        slope_x,
        slope_y,
    ) = terms
    lit = weights * residual * falloff
    grad_albedo = jnp.sum(lit * facing, axis=0)
    scaled = lit * albedo
    grad_direct = jnp.sum(scaled * (-1.0 + 3.0 * facing * delta_z / distance_sq), axis=0)
    grad_x = jnp.sum(scaled * (-delta_x - facing * slope_x / norm_sq), axis=0)
    grad_y = jnp.sum(scaled * (-delta_y - facing * slope_y / norm_sq), axis=0)
    return (grad_x, grad_y, grad_direct, grad_albedo)


def depth_stencil(grad_x_pad, grad_y_pad, grad_direct):
    return (
        grad_direct
        + 0.5 * (grad_x_pad[:, :-2] - grad_x_pad[:, 2:])
        + 0.5 * (grad_y_pad[:-2] - grad_y_pad[2:])
    )


def coordinates(nrows, total_rows, strip_cols):
    total_cols = strip_cols * lax.axis_size("strip")
    col_start = lax.axis_index("strip") * strip_cols
    columns = (jnp.arange(strip_cols) + col_start).astype(jnp.float32)
    coord_x = ((columns + 0.5) / total_cols - 0.5)[None, :]
    row_index = jnp.arange(nrows).astype(jnp.float32)
    coord_y = ((row_index + 0.5 - total_rows / 2.0) / total_cols)[:, None]
    return (coord_x, coord_y)


def update(surface, albedo, full_depth, full_albedo, mean_depth, mean_albedo):
    surface = surface - step_depth * jnp.tanh(full_depth / jnp.sqrt(mean_depth + epsilon))
    albedo = albedo - step_albedo * jnp.tanh(full_albedo / jnp.sqrt(mean_albedo + epsilon))
    return (surface, albedo)


def shards(depth_start, albedo_start, observations, light_table, valid_mask):
    strip_cols = depth_start.shape[1]
    total_rows = depth_start.shape[0]
    surface = depth_start
    albedo = albedo_start
    valid = valid_mask.astype(jnp.float32)
    coord_x, coord_y = coordinates(total_rows, total_rows, strip_cols)
    for iteration in range(ITERS):
        col_pad = extended(surface, (("strip", 1),), 1)
        row_pad = jnp.pad(surface, ((1, 1), (0, 0)))
        terms = shade_terms(
            surface, col_pad, row_pad, albedo, observations, light_table, valid, coord_x, coord_y
        )
        scores = terms[0]
        local_high = jnp.max(scores, axis=0)
        highest = lax.pmax(local_high, "light")
        raised = jnp.exp(scores - highest)
        summed = lax.psum(jnp.sum(raised, axis=0), "light")
        weights = raised / summed
        grad_x, grad_y, grad_direct, grad_albedo = light_gradients(weights, terms, albedo)
        grad_x, grad_y, grad_direct, full_albedo = lax.psum(
            (grad_x, grad_y, grad_direct, grad_albedo), "light"
        )
        slope_pad = extended(grad_x, (("strip", 1),), 1)
        full_depth = depth_stencil(slope_pad, jnp.pad(grad_y, ((1, 1), (0, 0))), grad_direct)
        square_depth, square_albedo = lax.psum(
            (jnp.sum(full_depth * full_depth), jnp.sum(full_albedo * full_albedo)), "strip"
        )
        pixel_count = full_depth.size * lax.axis_size("strip")
        surface, albedo = update(
            surface,
            albedo,
            full_depth,
            full_albedo,
            square_depth / pixel_count,
            square_albedo / pixel_count,
        )
    return (surface, albedo)


def solution(mesh):
    in_specs = (
        P(None, "strip"),
        P(None, "strip"),
        P("light", None, "strip"),
        P("light", None),
        P(None, "strip"),
    )
    out_specs = (P(None, "strip"), P(None, "strip"))
    return jax.shard_map(shards, mesh=mesh, in_specs=in_specs, out_specs=out_specs, check_vma=False)
```

profile of v0, /device:TPU:0, one launch (start us, length us, event | category | flops | bytes accessed | tf_op | source)
XLA Modules:
  0.0 334.7 jit_solution(5058168484332134036)
XLA Ops:
  9.6 5.5 %collective-permute-start.1 = (f32[128,1]{1,0:T(8,128)S(1)}, f32[128,1]{1,0:T(8,128)S(1)}, u32[]{:S(2)}, u32[]{:S(2)}) collective-permute-start(f32[128,1]{1,0:T(8,128)S(1)} %get-tuple-element.45), channel_id=1, source_target_pairs={{0,1},{1,2},{2,3},{3,4},{4,5},{5,6},{6,7},{8,9},{9,10},{10,11},{11... | collective-permute-start | bytes 1544 | tf_op jit(solution)/shard_map/ppermute | solution.py:18
  17.1 2.3 fusion.45
  20.2 2.7 fusion.15
  23.0 35.8 %all-reduce.15.cloned.1.call-done = f32[128,512]{1,0:T(8,128)} async-done(((f32[128,512]{1,0:T(8,128)}), f32[128,512]{1,0:T(8,128)}) %all-reduce.15.cloned.1.call-update) | async-done | bytes 262160 | tf_op jit(solution)/shard_map/pmax | solution.py:126
  58.9 2.1 fusion.14
  61.0 32.5 %all-reduce.17.cloned.1.call-done = f32[128,512]{1,0:T(8,128)} async-done(((f32[128,512]{1,0:T(8,128)}), f32[128,512]{1,0:T(8,128)}) %all-reduce.17.cloned.1.call-update) | async-done | bytes 262160 | tf_op jit(solution)/shard_map/psum | solution.py:128
  93.5 5.8 %multiply_reduce_fusion.5 = (f32[128,512]{1,0:T(8,128)}, f32[128,512]{1,0:T(8,128)}, f32[128,512]{1,0:T(8,128)}, f32[128,512]{1,0:T(8,128)}) fusion(f32[128,512]{1,0:T(8,128)} %get-tuple-element.35, f32[128,512]{1,0:T(8,128)} %copy-done.15, f32[8,512]{1,0:T(8,128)S(1)} %get-tuple-element.46, f32[8,128]{1,0:T(8,128)S(1)} %get-tuple-element.55, ...), kind=kLoop, calls=%fused_computation.33 | loop fusion | flops 18612224 | bytes 5566528 | tf_op jit(solution)/shard_map/reduce_sum | solution.py:82
  99.4 36.6 %all-reduce.25.cloned.1.call-done = (f32[128,512]{1,0:T(8,128)}, f32[128,512]{1,0:T(8,128)}, f32[128,512]{1,0:T(8,128)}, f32[128,512]{1,0:T(8,128)}) async-done(((f32[128,512]{1,0:T(8,128)}, f32[128,512]{1,0:T(8,128)}, f32[128,512]{1,0:T(8,128)}, f32[128,512]{1,0:T(8,128)}), (f32[128,512]{1,0:T(8,128)}, f32[128,512]{1,0:T(8,128)}, f32[128,512]{1,0:T(8,128)}, ...) | async-done | bytes 1048592 | tf_op jit(solution)/shard_map/psum | solution.py:131
  136.9 3.4 %collective-permute-start.2 = (f32[128,1]{1,0:T(8,128)S(1)}, f32[128,1]{1,0:T(8,128)S(1)}, u32[]{:S(2)}, u32[]{:S(2)}) collective-permute-start(f32[128,1]{1,0:T(8,128)S(1)} %get-tuple-element.42), channel_id=1, source_target_pairs={{0,1},{1,2},{2,3},{3,4},{4,5},{5,6},{6,7},{8,9},{9,10},{10,11},{11... | collective-permute-start | bytes 1544 | tf_op jit(solution)/shard_map/ppermute | solution.py:18
  143.2 3.2 collective-permute-done.3
  146.5 2.1 multiply_reduce_fusion.9
  148.6 20.2 %all-reduce.5 = (f32[]{:T(128)}, f32[]{:T(128)}) all-reduce(f32[]{:T(128)} %get-tuple-element.30, f32[]{:T(128)} %multiply_reduce_fusion.8), channel_id=1, replica_groups=mesh['light'=4,'strip'=8] {'strip'}, use_global_device_ids=true, to_apply=%region_11.12 | all-reduce | flops 2 | bytes 16 | tf_op jit(solution)/shard_map/psum | solution.py:136
  171.6 4.5 %collective-permute-start.5 = (f32[128,1]{1,0:T(8,128)S(1)}, f32[128,1]{1,0:T(8,128)S(1)}, u32[]{:S(2)}, u32[]{:S(2)}) collective-permute-start(f32[128,1]{1,0:T(8,128)S(1)} %get-tuple-element.41), channel_id=1, source_target_pairs={{0,1},{1,2},{2,3},{3,4},{4,5},{5,6},{6,7},{8,9},{9,10},{10,11},{11... | collective-permute-start | bytes 1544 | tf_op jit(solution)/shard_map/ppermute | solution.py:18
  179.7 4.0 %fusion.17 = (f32[128,512]{1,0:T(8,128)}, f32[8,128,512]{2,1,0:T(8,128)S(1)}) fusion(bf16[8,128,512]{2,1,0:T(8,128)(2,1)} %param.7, f32[8,128]{1,0:T(8,128)S(1)} %get-tuple-element.55, f32[128,512]{1,0:T(8,128)S(1)} %get-tuple-element.29, f32[8,512]{1,0:T(8,128)S(1)} %get-tuple-element.48, f32[128,512]{1,0:T(8,128)S(1)} %neg.27, ...), kind=kLoop, calls=%fused_computation.41 | loop fusion | flops 9895936 | bytes 5021760 | tf_op jit(solution)/shard_map/reduce_max | solution.py:125
  183.7 31.2 %all-reduce.19.cloned.1.call-done = f32[128,512]{1,0:T(8,128)} async-done(((f32[128,512]{1,0:T(8,128)}), f32[128,512]{1,0:T(8,128)}) %all-reduce.19.cloned.1.call-update) | async-done | bytes 262160 | tf_op jit(solution)/shard_map/pmax | solution.py:126
  214.9 2.1 fusion.16
  217.1 32.4 %all-reduce.21.cloned.1.call-done = f32[128,512]{1,0:T(8,128)} async-done(((f32[128,512]{1,0:T(8,128)}), f32[128,512]{1,0:T(8,128)}) %all-reduce.21.cloned.1.call-update) | async-done | bytes 262160 | tf_op jit(solution)/shard_map/psum | solution.py:128
  249.5 5.7 %multiply_reduce_fusion.2 = (f32[128,512]{1,0:T(8,128)}, f32[128,512]{1,0:T(8,128)}, f32[128,512]{1,0:T(8,128)}, f32[128,512]{1,0:T(8,128)}) fusion(f32[128,512]{1,0:T(8,128)} %get-tuple-element.27, f32[128,512]{1,0:T(8,128)} %copy-done.14, f32[128,512]{1,0:T(8,128)S(1)} %copy-done.9, f32[128,512]{1,0:T(8,128)S(1)} %neg.27, ...), kind=kLoop, calls=%fused_computation.28 | loop fusion | flops 18612224 | bytes 5566528 | tf_op jit(solution)/shard_map/reduce_sum | solution.py:82
  255.2 36.6 %all-reduce.23.cloned.1.call-done = (f32[128,512]{1,0:T(8,128)}, f32[128,512]{1,0:T(8,128)}, f32[128,512]{1,0:T(8,128)}, f32[128,512]{1,0:T(8,128)}) async-done(((f32[128,512]{1,0:T(8,128)}, f32[128,512]{1,0:T(8,128)}, f32[128,512]{1,0:T(8,128)}, f32[128,512]{1,0:T(8,128)}), (f32[128,512]{1,0:T(8,128)}, f32[128,512]{1,0:T(8,128)}, f32[128,512]{1,0:T(8,128)}, ...) | async-done | bytes 1048592 | tf_op jit(solution)/shard_map/psum | solution.py:131
  292.8 3.4 %collective-permute-start.6 = (f32[128,1]{1,0:T(8,128)S(1)}, f32[128,1]{1,0:T(8,128)S(1)}, u32[]{:S(2)}, u32[]{:S(2)}) collective-permute-start(f32[128,1]{1,0:T(8,128)S(1)} %get-tuple-element.38), channel_id=1, source_target_pairs={{0,1},{1,2},{2,3},{3,4},{4,5},{5,6},{6,7},{8,9},{9,10},{10,11},{11... | collective-permute-start | bytes 1544 | tf_op jit(solution)/shard_map/ppermute | solution.py:18
  299.1 3.2 collective-permute-done.7
  302.3 2.1 multiply_reduce_fusion.7
  304.4 20.2 %all-reduce.4 = (f32[]{:T(128)}, f32[]{:T(128)}) all-reduce(f32[]{:T(128)} %get-tuple-element.22, f32[]{:T(128)} %multiply_reduce_fusion.6), channel_id=1, replica_groups=mesh['light'=4,'strip'=8] {'strip'}, use_global_device_ids=true, to_apply=%region_27.28 | all-reduce | flops 2 | bytes 16 | tf_op jit(solution)/shard_map/psum | solution.py:136
  326.0 1.8 multiply_subtract_fusion
  (74 shorter events, 18.1 us)
Async XLA Ops:
  7.2 13.0 %copy-start = (f32[128,512]{1,0:T(8,128)S(1)}, f32[128,512]{1,0:T(8,128)}, u32[]{:S(2)}) copy-start(f32[128,512]{1,0:T(8,128)} %param.5) | copy-start | bytes 786436
  7.2 13.0 %copy-start.1 = (bf16[8,128,512]{2,1,0:T(8,128)(2,1)S(1)}, bf16[8,128,512]{2,1,0:T(8,128)(2,1)}, u32[]{:S(2)}) copy-start(bf16[8,128,512]{2,1,0:T(8,128)(2,1)} %param.7) | copy-start | bytes 3145732
  7.2 51.7 %all-reduce.15.cloned.1.call-start = ((), (), s32[]{:S(2)}) async-start(), calls=%async_computation | async-start | bytes 524288 | tf_op jit(solution)/shard_map/pmax | solution.py:126
  8.3 8.7 %collective-permute-start = (f32[128,1]{1,0:T(8,128)S(1)}, f32[128,1]{1,0:T(8,128)S(1)}, u32[]{:S(2)}, u32[]{:S(2)}) collective-permute-start(f32[128,1]{1,0:T(8,128)S(1)} %get-tuple-element.44), channel_id=1, source_target_pairs={{1,0},{2,1},{3,2},{4,3},{5,4},{6,5},{7,6},{9,8},{10,9},{11,10},{12... | collective-permute-start | bytes 1544 | tf_op jit(solution)/shard_map/ppermute | solution.py:21
  9.6 7.6 %collective-permute-start.1 = (f32[128,1]{1,0:T(8,128)S(1)}, f32[128,1]{1,0:T(8,128)S(1)}, u32[]{:S(2)}, u32[]{:S(2)}) collective-permute-start(f32[128,1]{1,0:T(8,128)S(1)} %get-tuple-element.45), channel_id=1, source_target_pairs={{0,1},{1,2},{2,3},{3,4},{4,5},{5,6},{6,7},{8,9},{9,10},{10,11},{11... | collective-permute-start | bytes 1544 | tf_op jit(solution)/shard_map/ppermute | solution.py:18
  17.0 5.9 %copy-start.2 = (f32[128,512]{1,0:T(8,128)}, f32[128,512]{1,0:T(8,128)S(1)}, u32[]{:S(2)}) copy-start(f32[128,512]{1,0:T(8,128)S(1)} %convert_element_type.30) | copy-start | bytes 786436
  22.9 70.6 %copy-start.7 = (f32[128,512]{1,0:T(8,128)S(1)}, f32[128,512]{1,0:T(8,128)}, u32[]{:S(2)}) copy-start(f32[128,512]{1,0:T(8,128)} %param.6) | copy-start | bytes 786436
  22.9 70.6 %copy-start.5 = (f32[128,512]{1,0:T(8,128)S(1)}, f32[128,512]{1,0:T(8,128)}, u32[]{:S(2)}) copy-start(f32[128,512]{1,0:T(8,128)} %copy-done.4) | copy-start | bytes 786436
  22.9 70.6 %copy-start.11 = (f32[128,512]{1,0:T(8,128)S(1)}, f32[128,512]{1,0:T(8,128)}, u32[]{:S(2)}) copy-start(f32[128,512]{1,0:T(8,128)} %copy-done.10) | copy-start | bytes 786436
  23.0 70.5 %copy-start.13 = (f32[128,512]{1,0:T(8,128)S(1)}, f32[128,512]{1,0:T(8,128)}, u32[]{:S(2)}) copy-start(f32[128,512]{1,0:T(8,128)} %copy-done.12) | copy-start | bytes 786436
  23.0 70.5 %all-reduce.17.cloned.1.call-start = ((), (), s32[]{:S(2)}) async-start(), calls=%async_computation.1 | async-start | bytes 524288 | tf_op jit(solution)/shard_map/psum | solution.py:128
  61.0 75.0 %all-reduce.25.cloned.1.call-start = ((), (), s32[]{:S(2)}) async-start(), calls=%async_computation.5 | async-start | bytes 2097152 | tf_op jit(solution)/shard_map/psum | solution.py:131
  99.3 115.6 %all-reduce.19.cloned.1.call-start = ((), (), s32[]{:S(2)}) async-start(), calls=%async_computation.2 | async-start | bytes 524288 | tf_op jit(solution)/shard_map/pmax | solution.py:126
  135.9 40.2 %copy-start.16 = (f32[128,512]{1,0:T(8,128)S(1)}, f32[128,512]{1,0:T(8,128)}, u32[]{:S(2)}) copy-start(f32[128,512]{1,0:T(8,128)} %get-tuple-element.21) | copy-start | bytes 786436
  136.9 6.3 %collective-permute-start.2 = (f32[128,1]{1,0:T(8,128)S(1)}, f32[128,1]{1,0:T(8,128)S(1)}, u32[]{:S(2)}, u32[]{:S(2)}) collective-permute-start(f32[128,1]{1,0:T(8,128)S(1)} %get-tuple-element.42), channel_id=1, source_target_pairs={{0,1},{1,2},{2,3},{3,4},{4,5},{5,6},{6,7},{8,9},{9,10},{10,11},{11... | collective-permute-start | bytes 1544 | tf_op jit(solution)/shard_map/ppermute | solution.py:18
  140.3 6.2 %collective-permute-start.3 = (f32[128,1]{1,0:T(8,128)S(1)}, f32[128,1]{1,0:T(8,128)S(1)}, u32[]{:S(2)}, u32[]{:S(2)}) collective-permute-start(f32[128,1]{1,0:T(8,128)S(1)} %get-tuple-element.43), channel_id=1, source_target_pairs={{1,0},{2,1},{3,2},{4,3},{5,4},{6,5},{7,6},{9,8},{10,9},{11,10},{12... | collective-permute-start | bytes 1544 | tf_op jit(solution)/shard_map/ppermute | solution.py:21
  148.6 31.1 %copy-start.3 = (f32[128,512]{1,0:T(8,128)S(1)}, f32[128,512]{1,0:T(8,128)}, u32[]{:S(2)}) copy-start(f32[128,512]{1,0:T(8,128)} %copy-done.2) | copy-start | bytes 786436
  170.3 6.2 %collective-permute-start.4 = (f32[128,1]{1,0:T(8,128)S(1)}, f32[128,1]{1,0:T(8,128)S(1)}, u32[]{:S(2)}, u32[]{:S(2)}) collective-permute-start(f32[128,1]{1,0:T(8,128)S(1)} %get-tuple-element.40), channel_id=1, source_target_pairs={{1,0},{2,1},{3,2},{4,3},{5,4},{6,5},{7,6},{9,8},{10,9},{11,10},{12... | collective-permute-start | bytes 1544 | tf_op jit(solution)/shard_map/ppermute | solution.py:21
  171.6 6.4 %collective-permute-start.5 = (f32[128,1]{1,0:T(8,128)S(1)}, f32[128,1]{1,0:T(8,128)S(1)}, u32[]{:S(2)}, u32[]{:S(2)}) collective-permute-start(f32[128,1]{1,0:T(8,128)S(1)} %get-tuple-element.41), channel_id=1, source_target_pairs={{0,1},{1,2},{2,3},{3,4},{4,5},{5,6},{6,7},{8,9},{9,10},{10,11},{11... | collective-permute-start | bytes 1544 | tf_op jit(solution)/shard_map/ppermute | solution.py:18
  183.7 65.8 %copy-start.9 = (f32[128,512]{1,0:T(8,128)S(1)}, f32[128,512]{1,0:T(8,128)}, u32[]{:S(2)}) copy-start(f32[128,512]{1,0:T(8,128)} %copy-done.8) | copy-start | bytes 786436
  183.7 65.8 %all-reduce.21.cloned.1.call-start = ((), (), s32[]{:S(2)}) async-start(), calls=%async_computation.3 | async-start | bytes 524288 | tf_op jit(solution)/shard_map/psum | solution.py:128
  217.0 74.8 %all-reduce.23.cloned.1.call-start = ((), (), s32[]{:S(2)}) async-start(), calls=%async_computation.4 | async-start | bytes 2097152 | tf_op jit(solution)/shard_map/psum | solution.py:131
  292.8 6.3 %collective-permute-start.6 = (f32[128,1]{1,0:T(8,128)S(1)}, f32[128,1]{1,0:T(8,128)S(1)}, u32[]{:S(2)}, u32[]{:S(2)}) collective-permute-start(f32[128,1]{1,0:T(8,128)S(1)} %get-tuple-element.38), channel_id=1, source_target_pairs={{0,1},{1,2},{2,3},{3,4},{4,5},{5,6},{6,7},{8,9},{9,10},{10,11},{11... | collective-permute-start | bytes 1544 | tf_op jit(solution)/shard_map/ppermute | solution.py:18
  296.2 6.2 %collective-permute-start.7 = (f32[128,1]{1,0:T(8,128)S(1)}, f32[128,1]{1,0:T(8,128)S(1)}, u32[]{:S(2)}, u32[]{:S(2)}) collective-permute-start(f32[128,1]{1,0:T(8,128)S(1)} %get-tuple-element.39), channel_id=1, source_target_pairs={{1,0},{2,1},{3,2},{4,3},{5,4},{6,5},{7,6},{9,8},{10,9},{11,10},{12... | collective-permute-start | bytes 1544 | tf_op jit(solution)/shard_map/ppermute | solution.py:21
  (7 other events, 21.4 us)
Sparse Core Ops, SparseCore 0:
  23.1 35.6 all-reduce.14
  61.2 32.2 all-reduce.16
  99.4 36.4 all-reduce.24
  183.8 31.0 all-reduce.18
  217.1 32.2 all-reduce.20
  255.3 36.4 all-reduce.22
where the time goes:
time: 336 us; the launch traced here: 335 us
  waiting for transfers between devices  214 us (64%)
  blocking collectives  40.4 us (12%)
  other arithmetic  37 us (11%)
  starting transfers between devices  22.2 us (7%)
  between operations  17.1 us (5%)
  local copies, waits for them, and re-layouts  4.48 us (1%)
    psum x2, waiting for transfers between devices, shards(): lax.psum((grad_x, grad_y, grad_direct, grad_albedo), 'light')  73.2 us
    pmax x2, waiting for transfers between devices, shards(): highest = lax.pmax(local_high, 'light')  67 us
    psum x2, waiting for transfers between devices, shards(): summed = lax.psum(jnp.sum(raised, axis=0), 'light')  64.9 us
    psum x2, blocking collectives, shards(): lax.psum((jnp.sum(full_depth * full_depth), jnp.sum(full_albedo * full_al...  40.4 us
    ppermute x4, starting transfers between devices, extended(): lax.ppermute(lax.slice_in_dim(block, block.shape[dim] - width, None, axis...  16.8 us
    reduce_sum x2, other arithmetic, light_gradients(): grad_x = jnp.sum(scaled * (-delta_x - facing * slope_x / norm_sq), axis=0)  11.5 us
  transfers between devices with their start and end apart: 14, of which 11 were waited for; matrix products, arithmetic and copies ran while one was open for 2% of the time, Pallas kernels for 0%

commit v1 on v0

--- a/solution.py
+++ b/solution.py
@@ -125,7 +125,7 @@
         local_high = jnp.max(scores, axis=0)
         highest = lax.pmax(local_high, "light")
         raised = jnp.exp(scores - highest)
-        summed = lax.psum(jnp.sum(raised, axis=0), "light")
+        summed = jnp.sum(lax.all_gather(jnp.sum(raised, axis=0), "light"), axis=0)
         weights = raised / summed
         grad_x, grad_y, grad_direct, grad_albedo = light_gradients(weights, terms, albedo)
         grad_x, grad_y, grad_direct, full_albedo = lax.psum(

time: 336 us -> 309 us (0.920)
  waiting for transfers between devices: 214 us -> 182 us
  other arithmetic: 37 us -> 41.3 us
    psum x2 -> x0, waiting for transfers between devices: 64.9 us -> none  [shards(): summed = lax.psum(jnp.sum(raised, axis=0), 'light')]
    all_gather x0 -> x2, waiting for transfers between devices: none -> 33.6 us  [shards(): summed = jnp.sum(lax.all_gather(jnp.sum(raised, axis=0), 'light'), axis=0)]
    reduce_sum x2 -> x4, other arithmetic: 4.16 us -> 8.39 us  [shards(): summed = jnp.sum(lax.all_gather(jnp.sum(raised, axis=0), 'light'), axis=0)]
where the time goes in v1:
time: 309 us; the launch traced here: 308 us
  waiting for transfers between devices  182 us (59%)
  other arithmetic  41.3 us (13%)
  blocking collectives  40.4 us (13%)
  starting transfers between devices  22.2 us (7%)
  between operations  17.1 us (6%)
  local copies, waits for them, and re-layouts  4.48 us (1%)
    psum x2, waiting for transfers between devices, shards(): lax.psum((grad_x, grad_y, grad_direct, grad_albedo), 'light')  73.1 us
    pmax x2, waiting for transfers between devices, shards(): highest = lax.pmax(local_high, 'light')  67 us
    psum x2, blocking collectives, shards(): lax.psum((jnp.sum(full_depth * full_depth), jnp.sum(full_albedo * full_al...  40.4 us
    all_gather x2, waiting for transfers between devices, shards(): summed = jnp.sum(lax.all_gather(jnp.sum(raised, axis=0), 'light'), axis=0)  33.6 us
    ppermute x4, starting transfers between devices, extended(): lax.ppermute(lax.slice_in_dim(block, block.shape[dim] - width, None, axis...  16.8 us
    reduce_sum x2, other arithmetic, light_gradients(): grad_x = jnp.sum(scaled * (-delta_x - facing * slope_x / norm_sq), axis=0)  11.5 us
    reduce_sum x4, other arithmetic, shards(): summed = jnp.sum(lax.all_gather(jnp.sum(raised, axis=0), 'light'), axis=0)  8.39 us
    reduce_max x2, other arithmetic, shards(): local_high = jnp.max(scores, axis=0)  6.72 us
  transfers between devices with their start and end apart: 14, of which 11 were waited for; matrix products, arithmetic and copies ran while one was open for 2% of the time, Pallas kernels for 0%

profile of v1, /device:TPU:0, one launch (start us, length us, event | category | flops | bytes accessed | tf_op | source)
XLA Modules:
  0.0 307.8 jit_solution(5121574028369564770)
XLA Ops:
  9.6 5.5 %collective-permute-start.1 = (f32[128,1]{1,0:T(8,128)S(1)}, f32[128,1]{1,0:T(8,128)S(1)}, u32[]{:S(2)}, u32[]{:S(2)}) collective-permute-start(f32[128,1]{1,0:T(8,128)S(1)} %get-tuple-element.45), channel_id=1, source_target_pairs={{0,1},{1,2},{2,3},{3,4},{4,5},{5,6},{6,7},{8,9},{9,10},{10,11},{11... | collective-permute-start | bytes 1544 | tf_op jit(solution)/shard_map/ppermute | solution.py:18
  17.1 2.4 fusion.45
  20.3 2.7 fusion.15
  23.1 35.8 %all-reduce.13.cloned.1.call-done = f32[128,512]{1,0:T(8,128)} async-done(((f32[128,512]{1,0:T(8,128)}), f32[128,512]{1,0:T(8,128)}) %all-reduce.13.cloned.1.call-update) | async-done | bytes 262160 | tf_op jit(solution)/shard_map/pmax | solution.py:126
  58.9 2.2 fusion.14
  61.2 16.8 %all-gather.5.cloned.1.call-done = f32[512,512]{1,0:T(8,128)} async-done(((f32[128,512]{1,0:T(8,128)}), f32[512,512]{1,0:T(8,128)}) %all-gather.5.cloned.1.call-update) | async-done | bytes 1048592 | tf_op jit(solution)/shard_map/all_gather | solution.py:128
  78.0 2.1 reduce_sum.145
  80.0 5.8 %multiply_reduce_fusion.5 = (f32[128,512]{1,0:T(8,128)}, f32[128,512]{1,0:T(8,128)}, f32[128,512]{1,0:T(8,128)}, f32[128,512]{1,0:T(8,128)}) fusion(f32[128,512]{1,0:T(8,128)} %get-tuple-element.35, f32[128,512]{1,0:T(8,128)} %copy-done.15, f32[8,512]{1,0:T(8,128)S(1)} %get-tuple-element.46, f32[8,128]{1,0:T(8,128)S(1)} %get-tuple-element.55, ...), kind=kLoop, calls=%fused_computation.33 | loop fusion | flops 18612224 | bytes 5566528 | tf_op jit(solution)/shard_map/reduce_sum | solution.py:82
  85.9 36.5 %all-reduce.19.cloned.1.call-done = (f32[128,512]{1,0:T(8,128)}, f32[128,512]{1,0:T(8,128)}, f32[128,512]{1,0:T(8,128)}, f32[128,512]{1,0:T(8,128)}) async-done(((f32[128,512]{1,0:T(8,128)}, f32[128,512]{1,0:T(8,128)}, f32[128,512]{1,0:T(8,128)}, f32[128,512]{1,0:T(8,128)}), (f32[128,512]{1,0:T(8,128)}, f32[128,512]{1,0:T(8,128)}, f32[128,512]{1,0:T(8,128)}, ...) | async-done | bytes 1048592 | tf_op jit(solution)/shard_map/psum | solution.py:131
  123.4 3.4 %collective-permute-start.2 = (f32[128,1]{1,0:T(8,128)S(1)}, f32[128,1]{1,0:T(8,128)S(1)}, u32[]{:S(2)}, u32[]{:S(2)}) collective-permute-start(f32[128,1]{1,0:T(8,128)S(1)} %get-tuple-element.42), channel_id=1, source_target_pairs={{0,1},{1,2},{2,3},{3,4},{4,5},{5,6},{6,7},{8,9},{9,10},{10,11},{11... | collective-permute-start | bytes 1544 | tf_op jit(solution)/shard_map/ppermute | solution.py:18
  129.8 3.2 %collective-permute-done.3 = f32[128,1]{1,0:T(8,128)S(1)} collective-permute-done((f32[128,1]{1,0:T(8,128)S(1)}, f32[128,1]{1,0:T(8,128)S(1)}, u32[]{:S(2)}, u32[]{:S(2)}) %collective-permute-start.3) | collective-permute-done | bytes 544 | tf_op jit(solution)/shard_map/ppermute | solution.py:21
  133.0 2.1 multiply_reduce_fusion.9
  135.1 20.2 %all-reduce.5 = (f32[]{:T(128)}, f32[]{:T(128)}) all-reduce(f32[]{:T(128)} %get-tuple-element.30, f32[]{:T(128)} %multiply_reduce_fusion.8), channel_id=1, replica_groups=mesh['light'=4,'strip'=8] {'strip'}, use_global_device_ids=true, to_apply=%region_11.12 | all-reduce | flops 2 | bytes 16 | tf_op jit(solution)/shard_map/psum | solution.py:136
  158.2 4.5 %collective-permute-start.5 = (f32[128,1]{1,0:T(8,128)S(1)}, f32[128,1]{1,0:T(8,128)S(1)}, u32[]{:S(2)}, u32[]{:S(2)}) collective-permute-start(f32[128,1]{1,0:T(8,128)S(1)} %get-tuple-element.41), channel_id=1, source_target_pairs={{0,1},{1,2},{2,3},{3,4},{4,5},{5,6},{6,7},{8,9},{9,10},{10,11},{11... | collective-permute-start | bytes 1544 | tf_op jit(solution)/shard_map/ppermute | solution.py:18
  166.3 4.0 %fusion.17 = (f32[128,512]{1,0:T(8,128)}, f32[8,128,512]{2,1,0:T(8,128)S(1)}) fusion(bf16[8,128,512]{2,1,0:T(8,128)(2,1)} %param.7, f32[8,128]{1,0:T(8,128)S(1)} %get-tuple-element.55, f32[128,512]{1,0:T(8,128)S(1)} %get-tuple-element.29, f32[8,512]{1,0:T(8,128)S(1)} %get-tuple-element.48, f32[128,512]{1,0:T(8,128)S(1)} %neg.27, ...), kind=kLoop, calls=%fused_computation.41 | loop fusion | flops 9895936 | bytes 5021760 | tf_op jit(solution)/shard_map/reduce_max | solution.py:125
  170.3 31.2 %all-reduce.15.cloned.1.call-done = f32[128,512]{1,0:T(8,128)} async-done(((f32[128,512]{1,0:T(8,128)}), f32[128,512]{1,0:T(8,128)}) %all-reduce.15.cloned.1.call-update) | async-done | bytes 262160 | tf_op jit(solution)/shard_map/pmax | solution.py:126
  201.5 2.1 fusion.16
  203.7 16.8 %all-gather.7.cloned.1.call-done = f32[512,512]{1,0:T(8,128)} async-done(((f32[128,512]{1,0:T(8,128)}), f32[512,512]{1,0:T(8,128)}) %all-gather.7.cloned.1.call-update) | async-done | bytes 1048592 | tf_op jit(solution)/shard_map/all_gather | solution.py:128
  222.5 5.7 %multiply_reduce_fusion.2 = (f32[128,512]{1,0:T(8,128)}, f32[128,512]{1,0:T(8,128)}, f32[128,512]{1,0:T(8,128)}, f32[128,512]{1,0:T(8,128)}) fusion(f32[128,512]{1,0:T(8,128)} %get-tuple-element.27, f32[128,512]{1,0:T(8,128)} %copy-done.14, f32[128,512]{1,0:T(8,128)S(1)} %copy-done.9, f32[128,512]{1,0:T(8,128)S(1)} %neg.27, ...), kind=kLoop, calls=%fused_computation.28 | loop fusion | flops 18612224 | bytes 5566528 | tf_op jit(solution)/shard_map/reduce_sum | solution.py:82
  228.3 36.6 %all-reduce.17.cloned.1.call-done = (f32[128,512]{1,0:T(8,128)}, f32[128,512]{1,0:T(8,128)}, f32[128,512]{1,0:T(8,128)}, f32[128,512]{1,0:T(8,128)}) async-done(((f32[128,512]{1,0:T(8,128)}, f32[128,512]{1,0:T(8,128)}, f32[128,512]{1,0:T(8,128)}, f32[128,512]{1,0:T(8,128)}), (f32[128,512]{1,0:T(8,128)}, f32[128,512]{1,0:T(8,128)}, f32[128,512]{1,0:T(8,128)}, ...) | async-done | bytes 1048592 | tf_op jit(solution)/shard_map/psum | solution.py:131
  265.8 3.4 %collective-permute-start.6 = (f32[128,1]{1,0:T(8,128)S(1)}, f32[128,1]{1,0:T(8,128)S(1)}, u32[]{:S(2)}, u32[]{:S(2)}) collective-permute-start(f32[128,1]{1,0:T(8,128)S(1)} %get-tuple-element.38), channel_id=1, source_target_pairs={{0,1},{1,2},{2,3},{3,4},{4,5},{5,6},{6,7},{8,9},{9,10},{10,11},{11... | collective-permute-start | bytes 1544 | tf_op jit(solution)/shard_map/ppermute | solution.py:18
  272.2 3.2 %collective-permute-done.7 = f32[128,1]{1,0:T(8,128)S(1)} collective-permute-done((f32[128,1]{1,0:T(8,128)S(1)}, f32[128,1]{1,0:T(8,128)S(1)}, u32[]{:S(2)}, u32[]{:S(2)}) %collective-permute-start.7) | collective-permute-done | bytes 544 | tf_op jit(solution)/shard_map/ppermute | solution.py:21
  275.4 2.1 multiply_reduce_fusion.7
  277.5 20.2 %all-reduce.4 = (f32[]{:T(128)}, f32[]{:T(128)}) all-reduce(f32[]{:T(128)} %get-tuple-element.22, f32[]{:T(128)} %multiply_reduce_fusion.6), channel_id=1, replica_groups=mesh['light'=4,'strip'=8] {'strip'}, use_global_device_ids=true, to_apply=%region_27.28 | all-reduce | flops 2 | bytes 16 | tf_op jit(solution)/shard_map/psum | solution.py:136
  (76 shorter events, 22.0 us)
Async XLA Ops:
  7.2 13.1 %copy-start = (f32[128,512]{1,0:T(8,128)S(1)}, f32[128,512]{1,0:T(8,128)}, u32[]{:S(2)}) copy-start(f32[128,512]{1,0:T(8,128)} %param.5) | copy-start | bytes 786436
  7.2 13.1 %copy-start.1 = (bf16[8,128,512]{2,1,0:T(8,128)(2,1)S(1)}, bf16[8,128,512]{2,1,0:T(8,128)(2,1)}, u32[]{:S(2)}) copy-start(bf16[8,128,512]{2,1,0:T(8,128)(2,1)} %param.7) | copy-start | bytes 3145732
  7.2 51.7 %all-reduce.13.cloned.1.call-start = ((), (), s32[]{:S(2)}) async-start(), calls=%async_computation | async-start | bytes 524288 | tf_op jit(solution)/shard_map/pmax | solution.py:126
  8.3 8.7 %collective-permute-start = (f32[128,1]{1,0:T(8,128)S(1)}, f32[128,1]{1,0:T(8,128)S(1)}, u32[]{:S(2)}, u32[]{:S(2)}) collective-permute-start(f32[128,1]{1,0:T(8,128)S(1)} %get-tuple-element.44), channel_id=1, source_target_pairs={{1,0},{2,1},{3,2},{4,3},{5,4},{6,5},{7,6},{9,8},{10,9},{11,10},{12... | collective-permute-start | bytes 1544 | tf_op jit(solution)/shard_map/ppermute | solution.py:21
  9.6 7.6 %collective-permute-start.1 = (f32[128,1]{1,0:T(8,128)S(1)}, f32[128,1]{1,0:T(8,128)S(1)}, u32[]{:S(2)}, u32[]{:S(2)}) collective-permute-start(f32[128,1]{1,0:T(8,128)S(1)} %get-tuple-element.45), channel_id=1, source_target_pairs={{0,1},{1,2},{2,3},{3,4},{4,5},{5,6},{6,7},{8,9},{9,10},{10,11},{11... | collective-permute-start | bytes 1544 | tf_op jit(solution)/shard_map/ppermute | solution.py:18
  17.0 6.0 %copy-start.2 = (f32[128,512]{1,0:T(8,128)}, f32[128,512]{1,0:T(8,128)S(1)}, u32[]{:S(2)}) copy-start(f32[128,512]{1,0:T(8,128)S(1)} %convert_element_type.30) | copy-start | bytes 786436
  23.0 54.9 %all-gather.5.cloned.1.call-start = ((), (), s32[]{:S(2)}) async-start(), calls=%async_computation.2 | async-start | bytes 1310720 | tf_op jit(solution)/shard_map/all_gather | solution.py:128
  58.9 21.1 %copy-start.5 = (f32[128,512]{1,0:T(8,128)S(1)}, f32[128,512]{1,0:T(8,128)}, u32[]{:S(2)}) copy-start(f32[128,512]{1,0:T(8,128)} %copy-done.4) | copy-start | bytes 786436
  58.9 21.1 %copy-start.7 = (f32[128,512]{1,0:T(8,128)S(1)}, f32[128,512]{1,0:T(8,128)}, u32[]{:S(2)}) copy-start(f32[128,512]{1,0:T(8,128)} %param.6) | copy-start | bytes 786436
  58.9 21.1 %copy-start.11 = (f32[128,512]{1,0:T(8,128)S(1)}, f32[128,512]{1,0:T(8,128)}, u32[]{:S(2)}) copy-start(f32[128,512]{1,0:T(8,128)} %copy-done.10) | copy-start | bytes 786436
  58.9 21.1 %copy-start.13 = (f32[128,512]{1,0:T(8,128)S(1)}, f32[128,512]{1,0:T(8,128)}, u32[]{:S(2)}) copy-start(f32[128,512]{1,0:T(8,128)} %copy-done.12) | copy-start | bytes 786436
  61.1 61.3 %all-reduce.19.cloned.1.call-start = ((), (), s32[]{:S(2)}) async-start(), calls=%async_computation.5 | async-start | bytes 2097152 | tf_op jit(solution)/shard_map/psum | solution.py:131
  85.8 115.6 %all-reduce.15.cloned.1.call-start = ((), (), s32[]{:S(2)}) async-start(), calls=%async_computation.1 | async-start | bytes 524288 | tf_op jit(solution)/shard_map/pmax | solution.py:126
  122.4 40.3 %copy-start.16 = (f32[128,512]{1,0:T(8,128)S(1)}, f32[128,512]{1,0:T(8,128)}, u32[]{:S(2)}) copy-start(f32[128,512]{1,0:T(8,128)} %get-tuple-element.21) | copy-start | bytes 786436
  123.4 6.3 %collective-permute-start.2 = (f32[128,1]{1,0:T(8,128)S(1)}, f32[128,1]{1,0:T(8,128)S(1)}, u32[]{:S(2)}, u32[]{:S(2)}) collective-permute-start(f32[128,1]{1,0:T(8,128)S(1)} %get-tuple-element.42), channel_id=1, source_target_pairs={{0,1},{1,2},{2,3},{3,4},{4,5},{5,6},{6,7},{8,9},{9,10},{10,11},{11... | collective-permute-start | bytes 1544 | tf_op jit(solution)/shard_map/ppermute | solution.py:18
  126.8 6.2 %collective-permute-start.3 = (f32[128,1]{1,0:T(8,128)S(1)}, f32[128,1]{1,0:T(8,128)S(1)}, u32[]{:S(2)}, u32[]{:S(2)}) collective-permute-start(f32[128,1]{1,0:T(8,128)S(1)} %get-tuple-element.43), channel_id=1, source_target_pairs={{1,0},{2,1},{3,2},{4,3},{5,4},{6,5},{7,6},{9,8},{10,9},{11,10},{12... | collective-permute-start | bytes 1544 | tf_op jit(solution)/shard_map/ppermute | solution.py:21
  135.1 31.1 %copy-start.3 = (f32[128,512]{1,0:T(8,128)S(1)}, f32[128,512]{1,0:T(8,128)}, u32[]{:S(2)}) copy-start(f32[128,512]{1,0:T(8,128)} %copy-done.2) | copy-start | bytes 786436
  156.9 6.2 %collective-permute-start.4 = (f32[128,1]{1,0:T(8,128)S(1)}, f32[128,1]{1,0:T(8,128)S(1)}, u32[]{:S(2)}, u32[]{:S(2)}) collective-permute-start(f32[128,1]{1,0:T(8,128)S(1)} %get-tuple-element.40), channel_id=1, source_target_pairs={{1,0},{2,1},{3,2},{4,3},{5,4},{6,5},{7,6},{9,8},{10,9},{11,10},{12... | collective-permute-start | bytes 1544 | tf_op jit(solution)/shard_map/ppermute | solution.py:21
  158.2 6.4 %collective-permute-start.5 = (f32[128,1]{1,0:T(8,128)S(1)}, f32[128,1]{1,0:T(8,128)S(1)}, u32[]{:S(2)}, u32[]{:S(2)}) collective-permute-start(f32[128,1]{1,0:T(8,128)S(1)} %get-tuple-element.41), channel_id=1, source_target_pairs={{0,1},{1,2},{2,3},{3,4},{4,5},{5,6},{6,7},{8,9},{9,10},{10,11},{11... | collective-permute-start | bytes 1544 | tf_op jit(solution)/shard_map/ppermute | solution.py:18
  170.3 50.2 %all-gather.7.cloned.1.call-start = ((), (), s32[]{:S(2)}) async-start(), calls=%async_computation.3 | async-start | bytes 1310720 | tf_op jit(solution)/shard_map/all_gather | solution.py:128
  201.5 21.0 %copy-start.9 = (f32[128,512]{1,0:T(8,128)S(1)}, f32[128,512]{1,0:T(8,128)}, u32[]{:S(2)}) copy-start(f32[128,512]{1,0:T(8,128)} %copy-done.8) | copy-start | bytes 786436
  203.6 61.3 %all-reduce.17.cloned.1.call-start = ((), (), s32[]{:S(2)}) async-start(), calls=%async_computation.4 | async-start | bytes 2097152 | tf_op jit(solution)/shard_map/psum | solution.py:131
  265.8 6.3 %collective-permute-start.6 = (f32[128,1]{1,0:T(8,128)S(1)}, f32[128,1]{1,0:T(8,128)S(1)}, u32[]{:S(2)}, u32[]{:S(2)}) collective-permute-start(f32[128,1]{1,0:T(8,128)S(1)} %get-tuple-element.38), channel_id=1, source_target_pairs={{0,1},{1,2},{2,3},{3,4},{4,5},{5,6},{6,7},{8,9},{9,10},{10,11},{11... | collective-permute-start | bytes 1544 | tf_op jit(solution)/shard_map/ppermute | solution.py:18
  269.2 6.2 %collective-permute-start.7 = (f32[128,1]{1,0:T(8,128)S(1)}, f32[128,1]{1,0:T(8,128)S(1)}, u32[]{:S(2)}, u32[]{:S(2)}) collective-permute-start(f32[128,1]{1,0:T(8,128)S(1)} %get-tuple-element.39), channel_id=1, source_target_pairs={{1,0},{2,1},{3,2},{4,3},{5,4},{6,5},{7,6},{9,8},{10,9},{11,10},{12... | collective-permute-start | bytes 1544 | tf_op jit(solution)/shard_map/ppermute | solution.py:21
  (7 other events, 21.6 us)
Sparse Core Ops, SparseCore 0:
  23.2 35.6 all-reduce.12
  61.2 16.6 all-gather.4
  86.0 36.4 all-reduce.18
  170.4 31.0 all-reduce.14
  203.8 16.6 all-gather.6
  228.4 36.4 all-reduce.16
